TPU v7x, 256 devices: a whole 4x4x8 slice. The times are simulated.
256 devices in a mesh: row: 16 (over z, x_lo), col: 16 (over x_hi, y, core).
Axes of the slice: x: 4 (x_hi: 2, x_lo: 2; x = x_hi * 2 + x_lo), y: 4, z: 8, core: 2. Of those that a mesh axis runs over, the one named last changes fastest.
Arguments:
- hidden: bfloat16 [196608, 6144], P(('row', 'col')), may hold values from -700 to 700
- gain: float32 [6144], replicated, may hold values from 0.5 to 1.5
- d_query: bfloat16 [196608, 512], P(('row', 'col')), may hold values from -0.03125 to 0.03125
Outputs:
- weight_grad: float32 [6144, 512], P('row')
All inputs are finite; a program needn't handle non-finite values.
Results may differ from a plain program's by a relative error of at most 0.0029.
Values sent between devices are 32-bit elements; how exact they have to be, the bound alone decides.
A program may use at most 64 MiB of HBM per device.

v0:
```python
import jax
import jax.numpy as jnp
from jax import lax
from jax.sharding import Mesh
from jax.sharding import PartitionSpec as P

ROW = ("row_0", "row_1")
ROW_COL = ("row_0", "row_1", "col")


def summed_rows(running, axes):
    for axis in axes:
        running = lax.psum_scatter(running, axis, scatter_dimension=0, tiled=True)
    return running


def per_device(hidden, gain, d_query):
    values = hidden.astype(jnp.float32)
    average = jnp.mean(values, axis=1, keepdims=True)
    centred = values - average
    spread = jnp.mean(centred * centred, axis=1, keepdims=True)
    normed = (centred * lax.rsqrt(spread + 1e-06) * gain).astype(jnp.bfloat16)
    partial_rows = summed_rows(
        lax.dot_general(
            normed, d_query, (((0,), (0,)), ((), ())), preferred_element_type=jnp.float32
        ),
        ROW,
    )
    result = lax.psum(partial_rows, "col")
    return result


def solution(mesh):
    split = Mesh(mesh.devices.reshape(8, 2, mesh.shape["col"]), ("row_0", "row_1", "col"))
    in_specs = (P(ROW_COL, None), P(), P(ROW_COL, None))
    out_specs = P(ROW, None)
    return jax.shard_map(
        per_device, mesh=split, in_specs=in_specs, out_specs=out_specs, check_vma=False
    )
```

profile of v0, /device:TPU:1, one launch (start us, length us, event | category | flops | bytes accessed | tf_op | source)
XLA Modules:
  0.0 353.4 jit_solution(16211676001173437454)
XLA Ops:
  6.5 0.0 copy-start
  6.5 0.0 reduce-scatter.3.cloned.1.call-start
  6.5 0.0 copy-start.1
  6.5 0.0 copy-start.2
  6.5 5.2 %convert_reduce_fusion = f32[768]{0:T(1024)S(1)} fusion(bf16[768,6144]{1,0:T(8,128)(2,1)} %param.3), kind=kLoop, calls=%fused_computation.1 | loop fusion | flops 9436416 | bytes 9440256 | tf_op jit(solution)/shard_map/reduce_sum | solution.py:19
  11.7 1.3 copy-done.1
  13.0 2.6 fusion.2
  15.6 0.0 copy-done
  15.6 0.0 copy-done.2
  15.6 9.7 %fusion.5 = f32[6144,512]{1,0:T(8,128)} fusion(bf16[768,512]{1,0:T(8,128)(2,1)S(1)} %copy-done, bf16[768,6144]{1,0:T(8,128)(2,1)S(1)} %copy-done.1, f32[6144]{0:T(1024)S(1)} %copy-done.2, f32[768]{0:T(1024)S(1)} %add_rsqrt_fusion, f32[768]{0:T(1024)S(1)} %broadcast_multiply_fusion), kind=kOutput, calls=%fused_computation.7 | convolution fusion | flops 4855431168 | bytes 22837248 | tf_op jit(solution)/shard_map/dot_general | solution.py:24
  25.3 0.0 reduce-scatter.3.cloned.1.call-update
  25.4 0.0 reduce-scatter.5.cloned.1.call-start
  25.4 138.5 %reduce-scatter.3.cloned.1.call-done = f32[768,512]{1,0:T(8,128)} async-done(((f32[6144,512]{1,0:T(8,128)}), f32[768,512]{1,0:T(8,128)}) %reduce-scatter.3.cloned.1.call-update) | async-done | bytes 1572880 | tf_op jit(solution)/shard_map/reduce_scatter | solution.py:13
  163.9 0.0 reduce-scatter.5.cloned.1.call-update
  163.9 0.0 all-reduce.2.cloned.1.call-start
  163.9 32.3 %reduce-scatter.5.cloned.1.call-done = f32[384,512]{1,0:T(8,128)} async-done(((f32[768,512]{1,0:T(8,128)}), f32[384,512]{1,0:T(8,128)}) %reduce-scatter.5.cloned.1.call-update) | async-done | bytes 786448 | tf_op jit(solution)/shard_map/reduce_scatter | solution.py:13
  196.3 0.0 all-reduce.2.cloned.1.call-update
  196.3 148.5 %all-reduce.2.cloned.1.call-done = f32[384,512]{1,0:T(8,128)} async-done(((f32[384,512]{1,0:T(8,128)}), f32[384,512]{1,0:T(8,128)}) %all-reduce.2.cloned.1.call-update) | async-done | bytes 786448 | tf_op jit(solution)/shard_map/psum | solution.py:29
  344.8 2.1 copy.5
  (2 shorter events, 0.0 us)
Async XLA Ops:
  6.5 9.0 %copy-start = (bf16[768,512]{1,0:T(8,128)(2,1)S(1)}, bf16[768,512]{1,0:T(8,128)(2,1)}, u32[]{:S(2)}) copy-start(bf16[768,512]{1,0:T(8,128)(2,1)} %param.5) | copy-start | bytes 2359300
  6.5 157.3 %reduce-scatter.3.cloned.1.call-start = ((), (), s32[]{:S(2)}) async-start(), calls=%async_computation.2 | async-start | bytes 14155776 | tf_op jit(solution)/shard_map/reduce_scatter | solution.py:13
  6.5 6.4 %copy-start.1 = (bf16[768,6144]{1,0:T(8,128)(2,1)S(1)}, bf16[768,6144]{1,0:T(8,128)(2,1)}, u32[]{:S(2)}) copy-start(bf16[768,6144]{1,0:T(8,128)(2,1)} %param.3) | copy-start | bytes 28311556
  6.5 9.0 %copy-start.2 = (f32[6144]{0:T(1024)S(1)}, f32[6144]{0:T(1024)}, u32[]{:S(2)}) copy-start(f32[6144]{0:T(1024)} %param.4) | copy-start | bytes 73732
  25.4 170.9 %reduce-scatter.5.cloned.1.call-start = ((), (), s32[]{:S(2)}) async-start(), calls=%async_computation.3 | async-start | bytes 2359296 | tf_op jit(solution)/shard_map/reduce_scatter | solution.py:13
  163.9 180.9 %all-reduce.2.cloned.1.call-start = ((), (), s32[]{:S(2)}) async-start(), calls=%async_computation.4 | async-start | bytes 1572864 | tf_op jit(solution)/shard_map/psum | solution.py:29
Sparse Core Ops, SparseCore 0:
  25.5 138.3 reduce-scatter.2
  166.4 29.8 reduce-scatter.4
  199.1 145.6 all-reduce.1
where the time goes:
time: 354 us; the launch traced here: 353 us
  waiting for transfers between devices  319 us (90%)
  between operations  13.1 us (4%)
  matrix products  9.74 us (3%)
  other arithmetic  7.76 us (2%)
    reduce_scatter x2, waiting for transfers between devices, summed_rows(): running = lax.psum_scatter(running, axis, scatter_dimension=0, tiled=True)  171 us
    psum x1, waiting for transfers between devices, per_device(): result = lax.psum(partial_rows, 'col')  149 us
    dot_general x1, matrix products, per_device(): lax.dot_general(normed, d_query, (((0,), (0,)), ((), ())), preferred_elem...  9.74 us
  transfers between devices with their start and end apart: 3, of which 3 were waited for; matrix products, arithmetic and copies ran while one was open for 0% of the time, Pallas kernels for 0%

commit v1 on v0

--- a/solution.py
+++ b/solution.py
@@ -26,7 +26,7 @@
         ),
         ROW,
     )
-    result = lax.psum(partial_rows, "col")
+    result = jnp.sum(lax.all_gather(partial_rows, "col"), axis=0)
     return result
 
 

time: 354 us -> 310 us (0.88)
  waiting for transfers between devices: 319 us -> 271 us
  other arithmetic: 7.76 us -> 14.8 us
    psum x1 -> x0, waiting for transfers between devices: 149 us -> none  [per_device(): result = lax.psum(partial_rows, 'col')]
    all_gather x0 -> x1, waiting for transfers between devices: none -> 100 us  [per_device(): result = jnp.sum(lax.all_gather(partial_rows, 'col'), axis=0)]
    reduce_sum x0 -> x1, other arithmetic: none -> 7.05 us  [per_device(): result = jnp.sum(lax.all_gather(partial_rows, 'col'), axis=0)]
where the time goes in v1:
time: 310 us
  waiting for transfers between devices  271 us (87%)
  other arithmetic  14.8 us (5%)
  between operations  13.1 us (4%)
  matrix products  9.74 us (3%)
    reduce_scatter x2, waiting for transfers between devices, summed_rows(): running = lax.psum_scatter(running, axis, scatter_dimension=0, tiled=True)  171 us
    all_gather x1, waiting for transfers between devices, per_device(): result = jnp.sum(lax.all_gather(partial_rows, 'col'), axis=0)  100 us
    dot_general x1, matrix products, per_device(): lax.dot_general(normed, d_query, (((0,), (0,)), ((), ())), preferred_elem...  9.74 us
    reduce_sum x1, other arithmetic, per_device(): result = jnp.sum(lax.all_gather(partial_rows, 'col'), axis=0)  7.05 us
  transfers between devices with their start and end apart: 3, of which 3 were waited for; matrix products, arithmetic and copies ran while one was open for 0% of the time, Pallas kernels for 0%

profile of v1, /device:TPU:1, one launch (start us, length us, event | category | flops | bytes accessed | tf_op | source)
XLA Modules:
  0.0 310.2 jit_solution(6398040233316129461)
XLA Ops:
  6.5 0.0 copy-start
  6.5 0.0 reduce-scatter.3.cloned.1.call-start
  6.5 0.0 copy-start.1
  6.5 0.0 copy-start.2
  6.5 5.2 %convert_reduce_fusion = f32[768]{0:T(1024)S(1)} fusion(bf16[768,6144]{1,0:T(8,128)(2,1)} %param.3), kind=kLoop, calls=%fused_computation.1 | loop fusion | flops 9436416 | bytes 9440256 | tf_op jit(solution)/shard_map/reduce_sum | solution.py:19
  11.7 1.3 copy-done.1
  13.0 2.6 fusion.2
  15.6 0.0 copy-done
  15.6 0.0 copy-done.2
  15.6 9.7 %fusion.5 = f32[6144,512]{1,0:T(8,128)} fusion(bf16[768,512]{1,0:T(8,128)(2,1)S(1)} %copy-done, bf16[768,6144]{1,0:T(8,128)(2,1)S(1)} %copy-done.1, f32[6144]{0:T(1024)S(1)} %copy-done.2, f32[768]{0:T(1024)S(1)} %add_rsqrt_fusion, f32[768]{0:T(1024)S(1)} %broadcast_multiply_fusion), kind=kOutput, calls=%fused_computation.7 | convolution fusion | flops 4855431168 | bytes 22837248 | tf_op jit(solution)/shard_map/dot_general | solution.py:24
  25.3 0.0 reduce-scatter.3.cloned.1.call-update
  25.4 0.0 reduce-scatter.5.cloned.1.call-start
  25.4 138.5 %reduce-scatter.3.cloned.1.call-done = f32[768,512]{1,0:T(8,128)} async-done(((f32[6144,512]{1,0:T(8,128)}), f32[768,512]{1,0:T(8,128)}) %reduce-scatter.3.cloned.1.call-update) | async-done | bytes 1572880 | tf_op jit(solution)/shard_map/reduce_scatter | solution.py:13
  163.9 0.0 reduce-scatter.5.cloned.1.call-update
  163.9 0.0 all-gather.3.cloned.1.call-start
  163.9 32.3 %reduce-scatter.5.cloned.1.call-done = f32[384,512]{1,0:T(8,128)} async-done(((f32[768,512]{1,0:T(8,128)}), f32[384,512]{1,0:T(8,128)}) %reduce-scatter.5.cloned.1.call-update) | async-done | bytes 786448 | tf_op jit(solution)/shard_map/reduce_scatter | solution.py:13
  196.3 0.0 all-gather.3.cloned.1.call-update
  196.3 100.4 %all-gather.3.cloned.1.call-done = f32[6144,512]{1,0:T(8,128)} async-done(((f32[384,512]{1,0:T(8,128)}), f32[6144,512]{1,0:T(8,128)}) %all-gather.3.cloned.1.call-update) | async-done | bytes 12582928 | tf_op jit(solution)/shard_map/all_gather | solution.py:29
  296.7 7.0 %reduce_sum.29 = f32[384,512]{1,0:T(8,128)} reduce(f32[16,384,512]{2,1,0:T(8,128)} %bitcast.2, f32[]{:T(128)} %constant.2.clone.1), dimensions={0}, to_apply=%region_4.0 | reduce | flops 2949120 | bytes 13369348 | tf_op jit(solution)/shard_map/reduce_sum | solution.py:29
  (2 shorter events, 0.0 us)
Async XLA Ops:
  6.5 9.0 %copy-start = (bf16[768,512]{1,0:T(8,128)(2,1)S(1)}, bf16[768,512]{1,0:T(8,128)(2,1)}, u32[]{:S(2)}) copy-start(bf16[768,512]{1,0:T(8,128)(2,1)} %param.5) | copy-start | bytes 2359300
  6.5 157.3 %reduce-scatter.3.cloned.1.call-start = ((), (), s32[]{:S(2)}) async-start(), calls=%async_computation.2 | async-start | bytes 14155776 | tf_op jit(solution)/shard_map/reduce_scatter | solution.py:13
  6.5 6.4 %copy-start.1 = (bf16[768,6144]{1,0:T(8,128)(2,1)S(1)}, bf16[768,6144]{1,0:T(8,128)(2,1)}, u32[]{:S(2)}) copy-start(bf16[768,6144]{1,0:T(8,128)(2,1)} %param.3) | copy-start | bytes 28311556
  6.5 9.0 %copy-start.2 = (f32[6144]{0:T(1024)S(1)}, f32[6144]{0:T(1024)}, u32[]{:S(2)}) copy-start(f32[6144]{0:T(1024)} %param.4) | copy-start | bytes 73732
  25.4 170.9 %reduce-scatter.5.cloned.1.call-start = ((), (), s32[]{:S(2)}) async-start(), calls=%async_computation.3 | async-start | bytes 2359296 | tf_op jit(solution)/shard_map/reduce_scatter | solution.py:13
  163.9 132.8 %all-gather.3.cloned.1.call-start = ((), (), s32[]{:S(2)}) async-start(), calls=%async_computation.4 | async-start | bytes 13369344 | tf_op jit(solution)/shard_map/all_gather | solution.py:29
Sparse Core Ops, SparseCore 0:
  25.5 138.3 reduce-scatter.2
  166.4 29.8 reduce-scatter.4
  199.4 97.1 all-gather.2
